TPU v7x, 512 devices: a whole 4x4x16 slice. The times are simulated.
512 devices in a mesh: section: 16 (over x, z_hi, core), tensor: 32 (over z_lo, y).
Axes of the slice: x: 4, y: 4, z: 16 (z_hi: 2, z_lo: 8; z = z_hi * 8 + z_lo), core: 2. Of those that a mesh axis runs over, the one named last changes fastest.
Arguments:
- context: bfloat16 [16, 256, 4096], P('section', None, 'tensor'), may hold values from -6 to 6
- out_weight: bfloat16 [16, 4096, 8192], P('section', 'tensor'), may hold values from -0.09375 to 0.09375
- residual: bfloat16 [16, 256, 8192], P('section', None, 'tensor'), may hold values from -36 to 36
- gain: float32 [16, 8192], P('section', 'tensor'), may hold values from 0.1 to 1.9
- q_weight: bfloat16 [16, 8192, 4096], P('section', None, 'tensor'), may hold values from -0.044194174 to 0.044194174
- kv_weight: bfloat16 [16, 8192, 1024], P('section', None, 'tensor'), may hold values from -0.044194174 to 0.044194174
Outputs:
- attended: bfloat16 [16, 256, 4096], P('section', None, 'tensor')
All inputs are finite; a program needn't handle non-finite values.
Results may differ from a plain program's by a relative error of at most 0.033.
Values may be sent and summed in bfloat16 or wider, within the bound.
No kernel may reach another device: no remote copies, remote signals or barrier semaphores. Data moves between devices by JAX's collectives and lax.ppermute only.
A program may use at most 64 MiB of HBM per device.

v0:
```python
import jax
import jax.numpy as jnp
from jax import lax
from jax.sharding import PartitionSpec as P

GROUP = 8
THETA = 500000.0


def passed_along(block, axis, distance):
    devices = range(lax.axis_size(axis))
    route = [((i - distance) % len(devices), i) for i in devices]
    return lax.ppermute(block, axis, route)


def rotate(inputs, positions):
    half_width = inputs.shape[-1] // 2
    frequency = THETA ** (-(jnp.arange(half_width).astype(jnp.float32) * 2.0 / inputs.shape[-1]))
    angles = positions[:, None] * frequency[None, :]
    cosine = jnp.cos(angles)[:, None, :]
    sine_part = jnp.sin(angles)[:, None, :]
    first_half = inputs[..., :half_width]
    second_half = inputs[..., half_width:]
    return jnp.concatenate(
        [
            first_half * cosine - second_half * sine_part,
            second_half * cosine + first_half * sine_part,
        ],
        axis=-1,
    )


def on_device(context, out_weight, residual, gain, q_weight, kv_weight):
    local_context = context[0]
    local_out = out_weight[0]
    terms = jnp.dot(local_context, local_out, preferred_element_type=jnp.float32)
    summed = lax.psum_scatter(
        terms.astype(jnp.bfloat16), "tensor", scatter_dimension=1, tiled=True
    ).astype(jnp.float32)
    combined = (residual[0].astype(jnp.float32) + summed).astype(jnp.bfloat16)
    section_gain = gain[0]
    query_cols = q_weight[0]
    pair_cols = kv_weight[0]
    head_size = query_cols.shape[1]
    length = combined.shape[0]
    gathered = lax.all_gather(combined, "tensor", axis=1, tiled=True)
    shifted = passed_along(gathered, "section", 1)
    full_gain = lax.all_gather(section_gain, "tensor", axis=0, tiled=True)
    values_f = shifted.astype(jnp.float32)
    normed = (
        values_f
        * lax.rsqrt(jnp.mean(values_f * values_f, axis=-1, keepdims=True) + 1e-05)
        * full_gain[None, :]
    ).astype(jnp.bfloat16)
    query_proj = jnp.dot(normed, query_cols, preferred_element_type=jnp.float32)
    pair_proj = jnp.dot(normed, pair_cols, preferred_element_type=jnp.float32)
    positions = jnp.arange(length).astype(jnp.float32)
    queries = rotate(query_proj[:, None, :], positions)[:, 0].astype(jnp.bfloat16)
    pair_part = pair_proj.astype(jnp.bfloat16)
    all_pairs = lax.all_gather(pair_part, "tensor", axis=1, tiled=True)
    group_count = lax.axis_size("tensor")
    feature_share = head_size // group_count
    kv_total = pair_cols.shape[1] * group_count // (2 * head_size)
    group_index = lax.axis_index("tensor") // GROUP
    split_cols = all_pairs.reshape(length, group_count, kv_total, 2 * feature_share)
    picked = lax.dynamic_index_in_dim(split_cols, group_index, 2, keepdims=False)
    picked = jnp.transpose(
        picked.reshape(length, group_count, 2, feature_share), (0, 2, 1, 3)
    ).reshape(length, 2, head_size)
    key_rows = rotate(picked[:, 0:1].astype(jnp.float32), positions)[:, 0].astype(jnp.bfloat16)
    values = picked[:, 1]
    scores = jnp.einsum(
        "sd,td->st", queries, key_rows, preferred_element_type=jnp.float32
    ) * head_size ** (-0.5)
    order = jnp.arange(length)
    causal = order[:, None] >= order[None, :]
    scores = jnp.where(causal, scores, -1e30)
    softmax_weights = jax.nn.softmax(scores, axis=-1).astype(jnp.bfloat16)
    attended = jnp.dot(softmax_weights, values, preferred_element_type=jnp.float32).astype(
        jnp.bfloat16
    )
    return attended[None]


def solution(mesh):
    placed = (
        P("section", None, "tensor"),
        P("section", "tensor", None),
        P("section", None, "tensor"),
        P("section", "tensor"),
        P("section", None, "tensor"),
        P("section", None, "tensor"),
    )
    return jax.shard_map(
        on_device,
        mesh=mesh,
        in_specs=placed,
        out_specs=P("section", None, "tensor"),
        check_vma=False,
    )
```

profile of v0, /device:TPU:1, one launch (start us, length us, event | category | flops | bytes accessed | tf_op | source)
XLA Modules:
  0.0 821.7 jit_solution(9606047402175932910)
XLA Ops:
  6.5 0.0 copy-start
  6.5 0.0 copy-start.1
  6.5 0.0 copy-start.2
  6.5 0.0 reduce-scatter.2.cloned.1.call-start
  6.5 1.6 copy-done
  8.1 4.0 convolution_convert_fusion
  12.1 0.0 copy-start.3
  12.1 0.0 reduce-scatter.2.cloned.1.call-update
  12.2 0.0 all-gather.3.cloned.1.call-start
  12.2 227.8 %reduce-scatter.2.cloned.1.call-done = bf16[256,256]{1,0:T(8,128)(2,1)} async-done(((bf16[256,8192]{1,0:T(8,128)(2,1)}), bf16[256,256]{1,0:T(8,128)(2,1)}) %reduce-scatter.2.cloned.1.call-update) | async-done | bytes 131088 | tf_op jit(solution)/shard_map/reduce_scatter | solution.py:37
  240.1 0.0 copy-done.1
  240.1 1.6 fusion.20
  241.7 0.0 all-gather.3.cloned.1.call-update
  241.7 193.1 %all-gather.3.cloned.1.call-done = bf16[256,8192]{1,0:T(8,128)(2,1)} async-done(((bf16[256,256]{1,0:T(8,128)(2,1)}), bf16[256,8192]{1,0:T(8,128)(2,1)}) %all-gather.3.cloned.1.call-update) | async-done | bytes 4194320 | tf_op jit(solution)/shard_map/all_gather | solution.py:46
  434.8 21.0 %collective-permute-start = (bf16[256,8192]{1,0:T(8,128)(2,1)}, bf16[256,8192]{1,0:T(8,128)(2,1)}, u32[]{:S(2)}, u32[]{:S(2)}) collective-permute-start(bf16[256,8192]{1,0:T(8,128)(2,1)} %all-gather.3.cloned.1.call-done), channel_id=1, source_target_pairs={{480,0},{0,32},{32,64},{64,96},{96,128},{128,160},{160,192},{192,2... | collective-permute-start | bytes 12582920 | tf_op jit(solution)/shard_map/ppermute | solution.py:13
  455.8 0.0 copy-done.2
  455.8 245.5 %all-gather = f32[1,8192]{1,0:T(1,128)S(1)} all-gather(f32[1,256]{1,0:T(1,128)S(1)} %copy-done.2), channel_id=2, replica_groups=mesh['section'=16,'tensor'=32] {'tensor'}, dimensions={1}, use_global_device_ids=true | all-gather | bytes 33792 | tf_op jit(solution)/shard_map/all_gather | solution.py:48
  701.3 0.0 collective-permute-done
  701.4 3.1 fusion
  704.5 0.0 copy-done.3
  704.5 3.6 fusion.16
  708.1 100.4 %all_gather.11 = bf16[256,1024]{0,1:T(8,128)(2,1)S(1)} all-gather(bf16[256,32]{0,1:T(8,128)(2,1)S(1)} %fusion.16), channel_id=1, replica_groups=mesh['section'=16,'tensor'=32] {'tensor'}, dimensions={1}, use_global_device_ids=true | all-gather | bytes 540672 | tf_op jit(solution)/shard_map/all_gather | solution.py:60
  808.5 0.1 copy.8
  808.7 4.6 fusion.10
  813.3 0.3 fusion.46
  813.7 0.3 fusion.50
  813.9 0.1 fusion.21
  814.0 0.9 fusion.15
  (7 shorter events, 0.1 us)
Async XLA Ops:
  6.5 1.6 copy-start
  6.5 233.5 %copy-start.1 = (bf16[1,256,256]{2,1,0:T(8,128)(2,1)S(1)}, bf16[1,256,256]{2,1,0:T(8,128)(2,1)}, u32[]{:S(2)}) copy-start(bf16[1,256,256]{2,1,0:T(8,128)(2,1)} %param.8) | copy-start | bytes 393220
  6.5 449.3 %copy-start.2 = (f32[1,256]{1,0:T(1,128)S(1)}, f32[1,256]{1,0:T(1,128)}, u32[]{:S(2)}) copy-start(f32[1,256]{1,0:T(1,128)} %param.9) | copy-start | bytes 3076
  6.5 233.5 %reduce-scatter.2.cloned.1.call-start = ((), (), s32[]{:S(2)}) async-start(), calls=%async_computation.1 | async-start | bytes 4325376 | tf_op jit(solution)/shard_map/reduce_scatter | solution.py:37
  12.1 692.3 %copy-start.3 = (bf16[1,8192,32]{1,2,0:T(8,128)(2,1)S(1)}, bf16[1,8192,32]{1,2,0:T(8,128)(2,1)}, u32[]{:S(2)}) copy-start(bf16[1,8192,32]{1,2,0:T(8,128)(2,1)} %param.11) | copy-start | bytes 1572868
  12.2 422.6 %all-gather.3.cloned.1.call-start = ((), (), s32[]{:S(2)}) async-start(), calls=%async_computation.2 | async-start | bytes 4325376 | tf_op jit(solution)/shard_map/all_gather | solution.py:46
  434.8 266.5 %collective-permute-start = (bf16[256,8192]{1,0:T(8,128)(2,1)}, bf16[256,8192]{1,0:T(8,128)(2,1)}, u32[]{:S(2)}, u32[]{:S(2)}) collective-permute-start(bf16[256,8192]{1,0:T(8,128)(2,1)} %all-gather.3.cloned.1.call-done), channel_id=1, source_target_pairs={{480,0},{0,32},{32,64},{64,96},{96,128},{128,160},{160,192},{192,2... | collective-permute-start | bytes 12582920 | tf_op jit(solution)/shard_map/ppermute | solution.py:13
Sparse Core Ops, SparseCore 0:
  12.3 227.7 reduce-scatter.1
  242.1 192.6 all-gather.2
where the time goes:
time: 822 us
  waiting for transfers between devices  421 us (51%)
  blocking collectives  346 us (42%)
  starting transfers between devices  21 us (3%)
  between operations  13.5 us (2%)
  matrix products  13.4 us (2%)
    all_gather x1, blocking collectives, on_device(): full_gain = lax.all_gather(section_gain, 'tensor', axis=0, tiled=True)  246 us
    reduce_scatter x1, waiting for transfers between devices, on_device(): lax.psum_scatter(terms.astype(jnp.bfloat16), 'tensor', scatter_dimension=...  228 us
    all_gather x1, waiting for transfers between devices, on_device(): gathered = lax.all_gather(combined, 'tensor', axis=1, tiled=True)  193 us
    all_gather x1, blocking collectives, on_device(): all_pairs = lax.all_gather(pair_part, 'tensor', axis=1, tiled=True)  100 us
    ppermute x1, starting transfers between devices, passed_along(): return lax.ppermute(block, axis, route)  21 us
  transfers between devices with their start and end apart: 3, of which 2 were waited for; matrix products, arithmetic and copies ran while one was open for 0% of the time, Pallas kernels for 0%

commit v1 on v0

--- a/solution.py
+++ b/solution.py
@@ -5,6 +5,19 @@
 
 GROUP = 8
 THETA = 500000.0
+
+
+def carry_vector_by_axis(w_in, d0=0):
+    tmp = jnp.concatenate(
+        jax.lax.all_to_all(
+            jnp.stack([w_in] * jax.lax.axis_size("tensor"), axis=0),
+            "tensor",
+            split_axis=0,
+            concat_axis=0,
+        ),
+        axis=d0,
+    )
+    return tmp
 
 
 def passed_along(block, axis, distance):
@@ -45,7 +58,7 @@
     length = combined.shape[0]
     gathered = lax.all_gather(combined, "tensor", axis=1, tiled=True)
     shifted = passed_along(gathered, "section", 1)
-    full_gain = lax.all_gather(section_gain, "tensor", axis=0, tiled=True)
+    full_gain = carry_vector_by_axis(section_gain)
     values_f = shifted.astype(jnp.float32)
     normed = (
         values_f

time: 822 us -> 765 us (0.931); the launches traced: 822 us -> 752 us
  blocking collectives: 346 us -> 107 us
  waiting for transfers between devices: 421 us -> 581 us
  starting transfers between devices: 21 us -> 30.1 us
    all_gather x1 -> x0, blocking collectives: 246 us -> none  [on_device(): full_gain = lax.all_gather(section_gain, 'tensor', axis=0, tiled=True)]
    ppermute x1, waiting for transfers between devices: 0.01 us -> 117 us  [passed_along(): return lax.ppermute(block, axis, route)]
    all_to_all x0 -> x1, waiting for transfers between devices: none -> 42.6 us  [carry_vector_by_axis(): jax.lax.all_to_all(jnp.stack([w_in] * jax.lax.axis_size('tensor'), axis=0...]
    all_to_all x0 -> x1, starting transfers between devices: none -> 9.11 us  [carry_vector_by_axis(): jax.lax.all_to_all(jnp.stack([w_in] * jax.lax.axis_size('tensor'), axis=0...]
  transfers between devices with their start and end apart: 3 -> 4, of which waited for: 2 -> 4; matrix products, arithmetic and copies ran while one was open for 0% -> 0% of each run, Pallas kernels for 0% -> 0%
where the time goes in v1:
time: 765 us; the launch traced here: 752 us
  waiting for transfers between devices  581 us (76%)
  blocking collectives  107 us (14%)
  starting transfers between devices  30.1 us (4%)
  between operations  13.5 us (2%)
  matrix products  13.4 us (2%)
    reduce_scatter x1, waiting for transfers between devices, on_device(): lax.psum_scatter(terms.astype(jnp.bfloat16), 'tensor', scatter_dimension=...  228 us
    all_gather x1, waiting for transfers between devices, on_device(): gathered = lax.all_gather(combined, 'tensor', axis=1, tiled=True)  193 us
    ppermute x1, waiting for transfers between devices, passed_along(): return lax.ppermute(block, axis, route)  117 us
    all_gather x1, blocking collectives, on_device(): all_pairs = lax.all_gather(pair_part, 'tensor', axis=1, tiled=True)  107 us
    all_to_all x1, waiting for transfers between devices, carry_vector_by_axis(): jax.lax.all_to_all(jnp.stack([w_in] * jax.lax.axis_size('tensor'), axis=0...  42.6 us
    ppermute x1, starting transfers between devices, passed_along(): return lax.ppermute(block, axis, route)  21 us
  transfers between devices with their start and end apart: 4, of which 4 were waited for; matrix products, arithmetic and copies ran while one was open for 0% of the time, Pallas kernels for 0%

profile of v1, /device:TPU:1, one launch (start us, length us, event | category | flops | bytes accessed | tf_op | source)
XLA Modules:
  0.0 752.2 jit_solution(1047605716893111867)
XLA Ops:
  6.5 0.0 copy-start
  6.5 0.0 copy-start.1
  6.5 0.0 copy-start.2
  6.5 0.0 reduce-scatter.2.cloned.1.call-start
  6.5 1.6 copy-done
  8.1 4.0 convolution_convert_fusion
  12.2 0.0 copy-start.3
  12.2 0.0 reduce-scatter.2.cloned.1.call-update
  12.2 0.0 all-gather.2.cloned.1.call-start
  12.2 227.8 %reduce-scatter.2.cloned.1.call-done = bf16[256,256]{1,0:T(8,128)(2,1)} async-done(((bf16[256,8192]{1,0:T(8,128)(2,1)}), bf16[256,256]{1,0:T(8,128)(2,1)}) %reduce-scatter.2.cloned.1.call-update) | async-done | bytes 131088 | tf_op jit(solution)/shard_map/reduce_scatter | solution.py:50
  240.1 0.0 copy-done.1
  240.1 1.6 fusion.20
  241.7 0.0 all-gather.2.cloned.1.call-update
  241.7 193.1 %all-gather.2.cloned.1.call-done = bf16[256,8192]{1,0:T(8,128)(2,1)} async-done(((bf16[256,256]{1,0:T(8,128)(2,1)}), bf16[256,8192]{1,0:T(8,128)(2,1)}) %all-gather.2.cloned.1.call-update) | async-done | bytes 4194320 | tf_op jit(solution)/shard_map/all_gather | solution.py:59
  434.8 21.0 %collective-permute-start = (bf16[256,8192]{1,0:T(8,128)(2,1)}, bf16[256,8192]{1,0:T(8,128)(2,1)}, u32[]{:S(2)}, u32[]{:S(2)}) collective-permute-start(bf16[256,8192]{1,0:T(8,128)(2,1)} %all-gather.2.cloned.1.call-done), channel_id=1, source_target_pairs={{480,0},{0,32},{32,64},{64,96},{96,128},{128,160},{160,192},{192,2... | collective-permute-start | bytes 12582920 | tf_op jit(solution)/shard_map/ppermute | solution.py:26
  455.8 0.0 copy-done.2
  455.8 0.6 stack.3
  456.4 9.1 %all-to-all-start = ((f32[32,1,256]{2,1,0:T(1,128)}), f32[32,1,256]{2,1,0:T(1,128)S(1)}, u32[]{:S(2)}, u32[]{:S(2)}) async-start(f32[32,1,256]{2,1,0:T(1,128)} %stack.3), calls=%async_computation.1 | async-start | bytes 65536 | tf_op jit(solution)/shard_map/all_to_all | solution.py:12
  465.6 117.3 %collective-permute-done = bf16[256,8192]{1,0:T(8,128)(2,1)} collective-permute-done((bf16[256,8192]{1,0:T(8,128)(2,1)}, bf16[256,8192]{1,0:T(8,128)(2,1)}, u32[]{:S(2)}, u32[]{:S(2)}) %collective-permute-start) | collective-permute-done | bytes 4194336 | tf_op jit(solution)/shard_map/ppermute | solution.py:26
  582.9 3.1 fusion
  586.0 42.6 %all-to-all-done = f32[32,1,256]{2,1,0:T(1,128)S(1)} async-done(((f32[32,1,256]{2,1,0:T(1,128)}), f32[32,1,256]{2,1,0:T(1,128)S(1)}, u32[]{:S(2)}, u32[]{:S(2)}) %all-to-all-start) | async-done | bytes 32800 | tf_op jit(solution)/shard_map/all_to_all | solution.py:12
  628.7 0.0 copy-done.3
  628.7 3.6 fusion.16
  632.2 106.7 %all_gather.7 = bf16[256,1024]{0,1:T(8,128)(2,1)S(1)} all-gather(bf16[256,32]{0,1:T(8,128)(2,1)S(1)} %fusion.16), channel_id=1, replica_groups=mesh['section'=16,'tensor'=32] {'tensor'}, dimensions={1}, use_global_device_ids=true | all-gather | bytes 540672 | tf_op jit(solution)/shard_map/all_gather | solution.py:73
  739.0 0.1 copy.8
  739.2 4.6 fusion.10
  743.8 0.3 fusion.46
  744.2 0.3 fusion.50
  744.4 0.1 fusion.21
  744.5 0.9 fusion.15
  (7 shorter events, 0.1 us)
Async XLA Ops:
  6.5 1.6 copy-start
  6.5 233.5 %copy-start.1 = (bf16[1,256,256]{2,1,0:T(8,128)(2,1)S(1)}, bf16[1,256,256]{2,1,0:T(8,128)(2,1)}, u32[]{:S(2)}) copy-start(bf16[1,256,256]{2,1,0:T(8,128)(2,1)} %param.8) | copy-start | bytes 393220
  6.5 449.2 %copy-start.2 = (f32[1,256]{1,0:T(1,128)S(1)}, f32[1,256]{1,0:T(1,128)}, u32[]{:S(2)}) copy-start(f32[1,256]{1,0:T(1,128)} %param.9) | copy-start | bytes 3076
  6.5 233.5 %reduce-scatter.2.cloned.1.call-start = ((), (), s32[]{:S(2)}) async-start(), calls=%async_computation.2 | async-start | bytes 4325376 | tf_op jit(solution)/shard_map/reduce_scatter | solution.py:50
  12.2 616.5 %copy-start.3 = (bf16[1,8192,32]{1,2,0:T(8,128)(2,1)S(1)}, bf16[1,8192,32]{1,2,0:T(8,128)(2,1)}, u32[]{:S(2)}) copy-start(bf16[1,8192,32]{1,2,0:T(8,128)(2,1)} %param.11) | copy-start | bytes 1572868
  12.2 422.6 %all-gather.2.cloned.1.call-start = ((), (), s32[]{:S(2)}) async-start(), calls=%async_computation.3 | async-start | bytes 4325376 | tf_op jit(solution)/shard_map/all_gather | solution.py:59
  434.8 148.1 %collective-permute-start = (bf16[256,8192]{1,0:T(8,128)(2,1)}, bf16[256,8192]{1,0:T(8,128)(2,1)}, u32[]{:S(2)}, u32[]{:S(2)}) collective-permute-start(bf16[256,8192]{1,0:T(8,128)(2,1)} %all-gather.2.cloned.1.call-done), channel_id=1, source_target_pairs={{480,0},{0,32},{32,64},{64,96},{96,128},{128,160},{160,192},{192,2... | collective-permute-start | bytes 12582920 | tf_op jit(solution)/shard_map/ppermute | solution.py:26
  456.4 172.2 %all-to-all-start = ((f32[32,1,256]{2,1,0:T(1,128)}), f32[32,1,256]{2,1,0:T(1,128)S(1)}, u32[]{:S(2)}, u32[]{:S(2)}) async-start(f32[32,1,256]{2,1,0:T(1,128)} %stack.3), calls=%async_computation.1 | async-start | bytes 65536 | tf_op jit(solution)/shard_map/all_to_all | solution.py:12
Sparse Core Ops, SparseCore 0:
  12.3 227.7 reduce-scatter.1
  242.1 192.6 all-gather.1
